TPU v7x, 32 devices: a whole 2x2x4 slice. The times are simulated.
32 devices in a mesh: replica: 8 (over z, core), group: 4 (over y, x).
Axes of the slice: x: 2, y: 2, z: 4, core: 2. Of those that a mesh axis runs over, the one named last changes fastest.
Arguments:
- tokens: bfloat16 [4096, 2048], P(('replica', 'group')), may hold values from -6 to 6
- lengths: int32 [8], P('replica'), may hold values from 128 to 512, as said below
- exit_layers: int32 [4096], P(('replica', 'group')), may hold values from 7 to 20, as said below
- pre_gain: bfloat16 [2048], P('group'), may hold values from 0.099609375 to 1.8984375
- pre_shift: bfloat16 [2048], P('group'), may hold values from -3 to 3
- query_weight: bfloat16 [2048, 2048], P('group'), may hold values from -0.1875 to 0.1875
- query_bias: bfloat16 [2048], P('group'), may hold values from -3 to 3
- key_weight: bfloat16 [2048, 2048], P('group'), may hold values from -0.1875 to 0.1875
- value_weight: bfloat16 [2048, 2048], P('group'), may hold values from -0.125 to 0.125
- value_bias: bfloat16 [2048], P('group'), may hold values from -3 to 3
- out_weight: bfloat16 [2048, 2048], P('group'), may hold values from -0.5 to 0.5
- out_bias: bfloat16 [2048], P('group'), may hold values from -1.75 to 1.75
- mid_gain: bfloat16 [2048], P('group'), may hold values from 0.099609375 to 1.8984375
- mid_shift: bfloat16 [2048], P('group'), may hold values from -3 to 3
- up_weight: bfloat16 [2048, 8192], P(None, 'group'), may hold values from -0.125 to 0.125
- up_bias: bfloat16 [8192], P('group'), may hold values from -3 to 3
- down_weight: bfloat16 [8192, 2048], P('group'), may hold values from -0.0625 to 0.0625
- down_bias: bfloat16 [2048], P('group'), may hold values from -1.75 to 1.75
- cotangent: bfloat16 [4096, 2048], P(('replica', 'group')), may hold values from -6 to 6
Outputs:
- output: bfloat16 [4096, 2048], P(('replica', 'group'))
- token_grad: bfloat16 [4096, 2048], P(('replica', 'group'))
- pre_gain_grad: float32 [2048], P('group')
- pre_shift_grad: float32 [2048], P('group')
- query_weight_grad: float32 [2048, 2048], P('group')
- query_bias_grad: float32 [2048], P('group')
- key_weight_grad: float32 [2048, 2048], P('group')
- value_weight_grad: float32 [2048, 2048], P('group')
- value_bias_grad: float32 [2048], P('group')
- out_weight_grad: float32 [2048, 2048], P('group')
- out_bias_grad: float32 [2048], P('group')
- mid_gain_grad: float32 [2048], P('group')
- mid_shift_grad: float32 [2048], P('group')
- up_weight_grad: float32 [2048, 8192], P(None, 'group')
- up_bias_grad: float32 [8192], P('group')
- down_weight_grad: float32 [8192, 2048], P('group')
- down_bias_grad: float32 [2048], P('group')
Inputs may be any that keep to these rules, and one draw needn't show every extreme that they name: `lengths`: some sequence has length 512 and some other has length 128. Within each sequence, exit_layers never rise from one position to the next.
All inputs are finite; a program needn't handle non-finite values.
Results may differ from a plain program's by a relative error of at most 0.02.
Values may be sent and summed in bfloat16 or wider, within the bound.
No kernel may reach another device: no remote copies, remote signals or barrier semaphores. Data moves between devices by JAX's collectives and lax.ppermute only.
A program may use at most 640 MiB of HBM per device.

v0:
```python
import jax
import jax.numpy as jnp
from jax import lax
from jax.sharding import PartitionSpec as P

D = 2048
H = 32
HD = 64
LAYER = 12


def layer_norm(values):
    center = values - jnp.mean(values, -1, keepdims=True)
    spread = jnp.mean(center * center, -1, keepdims=True)
    factor = lax.rsqrt(spread + 1e-05)
    return (center * factor, factor)


def norm_back(grad, normal, factor):
    return factor * (
        grad
        - jnp.mean(grad, -1, keepdims=True)
        - normal * jnp.mean(grad * normal, -1, keepdims=True)
    )


def gelu(values):
    return (
        0.5
        * values
        * (1.0 + jnp.tanh(0.7978845608 * (values + 0.044715 * values * values * values)))
    )


def gelu_back(values, grad):
    inner = 0.7978845608 * (values + 0.044715 * values * values * values)
    tangent = jnp.tanh(inner)
    slope = 0.5 * (1.0 + tangent) + 0.5 * values * (1.0 - tangent * tangent) * 0.7978845608 * (
        1.0 + 3.0 * 0.044715 * values * values
    )
    return grad * slope


def split_heads(matrix):
    groups = max(1, H // 8)
    return matrix.reshape(matrix.shape[0], groups, H // groups, HD).transpose(1, 0, 2, 3)


def join_heads(heads):
    return heads.transpose(1, 0, 2, 3).reshape(heads.shape[1], D)


def score_block(query_group, key_group, allowed):
    scores = (
        jnp.einsum("qhd,khd->hqk", query_group, key_group, preferred_element_type=jnp.float32)
        * 0.125
    )
    return jnp.where(allowed[None], scores, -1e30)


def matmul(left, right):
    return jnp.dot(left, right, preferred_element_type=jnp.float32)


def column_sums(matrix):
    return jnp.sum(matrix.astype(jnp.float32), 0)


def shards(
    tokens,
    lengths,
    exit_layers,
    pre_gain,
    pre_shift,
    query_weight,
    query_bias,
    key_weight,
    value_weight,
    value_bias,
    out_weight,
    out_bias,
    mid_gain,
    mid_shift,
    up_weight,
    up_bias,
    down_weight,
    down_bias,
    cotangent,
):
    local_rows = tokens.shape[0]
    group_count = lax.axis_size("group")
    seq_rows = local_rows * group_count
    member = lax.axis_index("group")
    position = member * local_rows + jnp.arange(local_rows, dtype=jnp.int32)
    active = ((position < lengths[0]) & (exit_layers > LAYER)).astype(jnp.float32)[:, None]
    allowed = jnp.arange(seq_rows, dtype=jnp.int32)[None, :] <= position[:, None]
    (
        gain_one,
        shift_one,
        gain_two,
        shift_two,
        query_full,
        key_full,
        value_full,
        out_full,
        qbias_full,
        vbias_full,
        obias_full,
    ) = (
        lax.all_gather(pre_gain, "group", axis=0, tiled=True),
        lax.all_gather(pre_shift, "group", axis=0, tiled=True),
        lax.all_gather(mid_gain, "group", axis=0, tiled=True),
        lax.all_gather(mid_shift, "group", axis=0, tiled=True),
        lax.all_gather(query_weight, "group", axis=0, tiled=True),
        lax.all_gather(key_weight, "group", axis=0, tiled=True),
        lax.all_gather(value_weight, "group", axis=0, tiled=True),
        lax.all_gather(out_weight, "group", axis=0, tiled=True),
        lax.all_gather(query_bias, "group", axis=0, tiled=True),
        lax.all_gather(value_bias, "group", axis=0, tiled=True),
        lax.all_gather(out_bias, "group", axis=0, tiled=True),
    )
    inputs = tokens.astype(jnp.float32)
    normed_one, factor_one = layer_norm(inputs)
    attn_in = (normed_one * gain_one.astype(jnp.float32) + shift_one.astype(jnp.float32)).astype(
        jnp.bfloat16
    )
    queries = (matmul(attn_in, query_full) + qbias_full.astype(jnp.float32)).astype(jnp.bfloat16)
    keys_local = matmul(attn_in, key_full).astype(jnp.bfloat16)
    values_local = (matmul(attn_in, value_full) + vbias_full.astype(jnp.float32)).astype(
        jnp.bfloat16
    )
    keys_all, values_all = (
        lax.all_gather(keys_local, "group", axis=0, tiled=True),
        lax.all_gather(values_local, "group", axis=0, tiled=True),
    )
    query_heads = split_heads(queries)
    key_heads = split_heads(keys_all)
    value_heads = split_heads(values_all)

    def forward_group(operands):
        query_group, key_group, value_group = operands
        scores = score_block(query_group, key_group, allowed)
        top = jnp.max(scores, -1, keepdims=True)
        logsum = top + jnp.log(jnp.sum(jnp.exp(scores - top), -1, keepdims=True))
        weights = jnp.exp(scores - logsum).astype(jnp.bfloat16)
        context_part = jnp.einsum(
            "hqk,khd->qhd", weights, value_group, preferred_element_type=jnp.float32
        )
        return (context_part, logsum[..., 0])

    context_heads, logsums = lax.map(forward_group, (query_heads, key_heads, value_heads))
    context_low = join_heads(context_heads).astype(jnp.bfloat16)
    attn_out = matmul(context_low, out_full) + obias_full.astype(jnp.float32)
    hidden = inputs + active * attn_out
    normed_two, factor_two = layer_norm(hidden)
    ffn_in = (normed_two * gain_two.astype(jnp.float32) + shift_two.astype(jnp.float32)).astype(
        jnp.bfloat16
    )
    up_full, upbias_full, down_full, downbias_full = (
        lax.all_gather(up_weight, "group", axis=1, tiled=True),
        lax.all_gather(up_bias, "group", axis=0, tiled=True),
        lax.all_gather(down_weight, "group", axis=0, tiled=True),
        lax.all_gather(down_bias, "group", axis=0, tiled=True),
    )
    pre_act = matmul(ffn_in, up_full) + upbias_full.astype(jnp.float32)
    act_low = gelu(pre_act).astype(jnp.bfloat16)
    branch = matmul(act_low, down_full) + downbias_full.astype(jnp.float32)
    output = (hidden + active * branch).astype(jnp.bfloat16)
    first_gain, second_gain, query_back, key_back, value_back, out_back = (
        lax.all_gather(pre_gain, "group", axis=0, tiled=True),
        lax.all_gather(mid_gain, "group", axis=0, tiled=True),
        lax.all_gather(query_weight, "group", axis=0, tiled=True),
        lax.all_gather(key_weight, "group", axis=0, tiled=True),
        lax.all_gather(value_weight, "group", axis=0, tiled=True),
        lax.all_gather(out_weight, "group", axis=0, tiled=True),
    )
    grad_out = cotangent.astype(jnp.float32)
    branch_grad = (active * grad_out).astype(jnp.bfloat16)
    up_back, down_back = (
        lax.all_gather(up_weight, "group", axis=1, tiled=True),
        lax.all_gather(down_weight, "group", axis=0, tiled=True),
    )
    act_grad = matmul(branch_grad, down_back.T)
    pre_grad = gelu_back(pre_act, act_grad).astype(jnp.bfloat16)
    ffn_in_grad = matmul(pre_grad, up_back.T)
    up_grad, up_bias_grad, down_grad, down_bias_grad = (
        lax.psum_scatter(
            matmul(ffn_in.T, pre_grad).astype(jnp.bfloat16),
            "group",
            scatter_dimension=1,
            tiled=True,
        ).astype(jnp.float32),
        lax.psum_scatter(
            column_sums(pre_grad).astype(jnp.bfloat16), "group", scatter_dimension=0, tiled=True
        ).astype(jnp.float32),
        lax.psum_scatter(
            matmul(act_low.T, branch_grad).astype(jnp.bfloat16),
            "group",
            scatter_dimension=0,
            tiled=True,
        ).astype(jnp.float32),
        lax.psum_scatter(
            column_sums(branch_grad).astype(jnp.bfloat16), "group", scatter_dimension=0, tiled=True
        ).astype(jnp.float32),
    )
    mid_gain_part = jnp.sum(ffn_in_grad * normed_two, 0)
    mid_shift_part = jnp.sum(ffn_in_grad, 0)
    hidden_grad = grad_out + norm_back(
        ffn_in_grad * second_gain.astype(jnp.float32), normed_two, factor_two
    )
    attn_grad = (active * hidden_grad).astype(jnp.bfloat16)
    context_grad = matmul(attn_grad, out_back.T).astype(jnp.bfloat16)
    out_bias_part = column_sums(attn_grad)

    def backward_group(operands):
        query_group, key_group, value_group, grad_group, logsum_group = operands
        scores = score_block(query_group, key_group, allowed)
        probs = jnp.exp(scores - logsum_group[..., None])
        probs_grad = jnp.einsum(
            "qhd,khd->hqk", grad_group, value_group, preferred_element_type=jnp.float32
        )
        delta = jnp.sum(probs * probs_grad, -1, keepdims=True)
        score_grad = (probs * (probs_grad - delta)).astype(jnp.bfloat16)
        query_part = (
            jnp.einsum("hqk,khd->qhd", score_grad, key_group, preferred_element_type=jnp.float32)
            * 0.125
        )
        key_part = (
            jnp.einsum("hqk,qhd->khd", score_grad, query_group, preferred_element_type=jnp.float32)
            * 0.125
        )
        value_part = jnp.einsum(
            "hqk,qhd->khd",
            probs.astype(jnp.bfloat16),
            grad_group,
            preferred_element_type=jnp.float32,
        )
        return (query_part, key_part, value_part)

    query_parts, key_parts, value_parts = lax.map(
        backward_group, (query_heads, key_heads, value_heads, split_heads(context_grad), logsums)
    )
    query_grad = join_heads(query_parts).astype(jnp.bfloat16)
    key_sum, value_sum = (
        lax.psum_scatter(
            join_heads(key_parts).astype(jnp.bfloat16), "group", scatter_dimension=0, tiled=True
        ).astype(jnp.float32),
        lax.psum_scatter(
            join_heads(value_parts).astype(jnp.bfloat16), "group", scatter_dimension=0, tiled=True
        ).astype(jnp.float32),
    )
    key_grad = key_sum.astype(jnp.bfloat16)
    value_grad = value_sum.astype(jnp.bfloat16)
    in_grad = (
        matmul(query_grad, query_back.T)
        + matmul(key_grad, key_back.T)
        + matmul(value_grad, value_back.T)
    )
    pre_gain_part = jnp.sum(in_grad * normed_one, 0)
    pre_shift_part = jnp.sum(in_grad, 0)
    token_grad = (
        hidden_grad + norm_back(in_grad * first_gain.astype(jnp.float32), normed_one, factor_one)
    ).astype(jnp.bfloat16)
    (
        pre_gain_grad,
        pre_shift_grad,
        mid_gain_grad,
        mid_shift_grad,
        query_wgrad,
        key_wgrad,
        value_wgrad,
        out_wgrad,
        query_bgrad,
        value_bgrad,
        out_bgrad,
    ) = (
        lax.psum_scatter(
            pre_gain_part.astype(jnp.bfloat16), "group", scatter_dimension=0, tiled=True
        ).astype(jnp.float32),
        lax.psum_scatter(
            pre_shift_part.astype(jnp.bfloat16), "group", scatter_dimension=0, tiled=True
        ).astype(jnp.float32),
        lax.psum_scatter(
            mid_gain_part.astype(jnp.bfloat16), "group", scatter_dimension=0, tiled=True
        ).astype(jnp.float32),
        lax.psum_scatter(
            mid_shift_part.astype(jnp.bfloat16), "group", scatter_dimension=0, tiled=True
        ).astype(jnp.float32),
        lax.psum_scatter(
            matmul(attn_in.T, query_grad).astype(jnp.bfloat16),
            "group",
            scatter_dimension=0,
            tiled=True,
        ).astype(jnp.float32),
        lax.psum_scatter(
            matmul(attn_in.T, key_grad).astype(jnp.bfloat16),
            "group",
            scatter_dimension=0,
            tiled=True,
        ).astype(jnp.float32),
        lax.psum_scatter(
            matmul(attn_in.T, value_grad).astype(jnp.bfloat16),
            "group",
            scatter_dimension=0,
            tiled=True,
        ).astype(jnp.float32),
        lax.psum_scatter(
            matmul(context_low.T, attn_grad).astype(jnp.bfloat16),
            "group",
            scatter_dimension=0,
            tiled=True,
        ).astype(jnp.float32),
        lax.psum_scatter(
            column_sums(query_grad).astype(jnp.bfloat16), "group", scatter_dimension=0, tiled=True
        ).astype(jnp.float32),
        lax.psum_scatter(
            column_sums(value_grad).astype(jnp.bfloat16), "group", scatter_dimension=0, tiled=True
        ).astype(jnp.float32),
        lax.psum_scatter(
            out_bias_part.astype(jnp.bfloat16), "group", scatter_dimension=0, tiled=True
        ).astype(jnp.float32),
    )
    totals = (
        lax.psum(pre_gain_grad.astype(jnp.bfloat16), "replica").astype(jnp.float32),
        lax.psum(pre_shift_grad.astype(jnp.bfloat16), "replica").astype(jnp.float32),
        lax.psum(query_wgrad.astype(jnp.bfloat16), "replica").astype(jnp.float32),
        lax.psum(query_bgrad.astype(jnp.bfloat16), "replica").astype(jnp.float32),
        lax.psum(key_wgrad.astype(jnp.bfloat16), "replica").astype(jnp.float32),
        lax.psum(value_wgrad.astype(jnp.bfloat16), "replica").astype(jnp.float32),
        lax.psum(value_bgrad.astype(jnp.bfloat16), "replica").astype(jnp.float32),
        lax.psum(out_wgrad.astype(jnp.bfloat16), "replica").astype(jnp.float32),
        lax.psum(out_bgrad.astype(jnp.bfloat16), "replica").astype(jnp.float32),
        lax.psum(mid_gain_grad.astype(jnp.bfloat16), "replica").astype(jnp.float32),
        lax.psum(mid_shift_grad.astype(jnp.bfloat16), "replica").astype(jnp.float32),
        lax.psum(up_grad.astype(jnp.bfloat16), "replica").astype(jnp.float32),
        lax.psum(up_bias_grad.astype(jnp.bfloat16), "replica").astype(jnp.float32),
        lax.psum(down_grad.astype(jnp.bfloat16), "replica").astype(jnp.float32),
        lax.psum(down_bias_grad.astype(jnp.bfloat16), "replica").astype(jnp.float32),
    )
    return (
        output,
        token_grad,
        totals[0],
        totals[1],
        totals[2],
        totals[3],
        totals[4],
        totals[5],
        totals[6],
        totals[7],
        totals[8],
        totals[9],
        totals[10],
        totals[11],
        totals[12],
        totals[13],
        totals[14],
    )


def solution(mesh):
    return jax.shard_map(
        shards,
        mesh=mesh,
        in_specs=(
            P(("replica", "group"), None),
            P("replica"),
            P(("replica", "group")),
            P("group"),
            P("group"),
            P("group", None),
            P("group"),
            P("group", None),
            P("group", None),
            P("group"),
            P("group", None),
            P("group"),
            P("group"),
            P("group"),
            P(None, "group"),
            P("group"),
            P("group", None),
            P("group"),
            P(("replica", "group"), None),
        ),
        out_specs=(
            P(("replica", "group"), None),
            P(("replica", "group"), None),
            P("group"),
            P("group"),
            P("group", None),
            P("group"),
            P("group", None),
            P("group", None),
            P("group"),
            P("group", None),
            P("group"),
            P("group"),
            P("group"),
            P(None, "group"),
            P("group"),
            P("group", None),
            P("group"),
        ),
        check_vma=False,
    )
```

profile of v0, /device:TPU:0, one launch (start us, length us, event | category | flops | bytes accessed | tf_op | source)
XLA Modules:
  0.0 2687.4 jit_solution(7998907598796842740)
XLA Ops:
  34.8 65.6 %all-gather.17.cloned.1.call-done = bf16[2048,2048]{1,0:T(8,128)(2,1)} async-done(((bf16[512,2048]{1,0:T(8,128)(2,1)}), bf16[2048,2048]{1,0:T(8,128)(2,1)}) %all-gather.17.cloned.1.call-update) | async-done | bytes 8388624 | tf_op jit(solution)/shard_map/all_gather | solution.py:116
  105.9 83.9 %all-gather.23.cloned.1.call-done = bf16[2048,2048]{1,0:T(8,128)(2,1)} async-done(((bf16[512,2048]{1,0:T(8,128)(2,1)}), bf16[2048,2048]{1,0:T(8,128)(2,1)}) %all-gather.23.cloned.1.call-update) | async-done | bytes 8388624 | tf_op jit(solution)/shard_map/all_gather | solution.py:115
  237.1 42.5 %all-gather.21.cloned.1.call-done = bf16[2048,2048]{1,0:T(8,128)(2,1)} async-done(((bf16[512,2048]{1,0:T(8,128)(2,1)}), bf16[2048,2048]{1,0:T(8,128)(2,1)}) %all-gather.21.cloned.1.call-update) | async-done | bytes 8388624 | tf_op jit(solution)/shard_map/all_gather | solution.py:114
  284.6 32.6 %all-gather.19.cloned.1.call-done = bf16[512,2048]{1,0:T(8,128)(2,1)} async-done(((bf16[128,2048]{1,0:T(8,128)(2,1)}), bf16[512,2048]{1,0:T(8,128)(2,1)}) %all-gather.19.cloned.1.call-update) | async-done | bytes 2097168 | tf_op jit(solution)/shard_map/all_gather | solution.py:134
  321.3 33.5 %all-gather.25.cloned.1.call-done = bf16[512,2048]{1,0:T(8,128)(2,1)} async-done(((bf16[128,2048]{1,0:T(8,128)(2,1)}), bf16[512,2048]{1,0:T(8,128)(2,1)}) %all-gather.25.cloned.1.call-update) | async-done | bytes 2097168 | tf_op jit(solution)/shard_map/all_gather | solution.py:133
  374.4 69.8 %all-gather.27.cloned.1.call-done = bf16[2048,2048]{1,0:T(8,128)(2,1)} async-done(((bf16[512,2048]{1,0:T(8,128)(2,1)}), bf16[2048,2048]{1,0:T(8,128)(2,1)}) %all-gather.27.cloned.1.call-update) | async-done | bytes 8388624 | tf_op jit(solution)/shard_map/all_gather | solution.py:117
  450.3 292.9 %all-gather.29.cloned.1.call-done = bf16[2048,8192]{1,0:T(8,128)(2,1)} async-done(((bf16[2048,2048]{1,0:T(8,128)(2,1)}), bf16[2048,8192]{1,0:T(8,128)(2,1)}) %all-gather.29.cloned.1.call-update) | async-done | bytes 33554448 | tf_op jit(solution)/shard_map/all_gather | solution.py:160
  743.3 20.8 convolution_add_fusion
  764.0 278.3 %all-gather.31.cloned.1.call-done = bf16[8192,2048]{1,0:T(8,128)(2,1)} async-done(((bf16[2048,2048]{1,0:T(8,128)(2,1)}), bf16[8192,2048]{1,0:T(8,128)(2,1)}) %all-gather.31.cloned.1.call-update) | async-done | bytes 33554448 | tf_op jit(solution)/shard_map/all_gather | solution.py:162
  1042.3 18.8 fusion.81
  1061.2 19.7 multiply_reduce_fusion.1
  1095.0 31.3 %while.29 = (s32[]{:T(128)}, bf16[4,128,8,64]{1,3,2,0:T(8,128)(2,1)}, bf16[4,512,8,64]{1,3,2,0:T(8,128)(2,1)}, bf16[4,512,8,64]{1,3,2,0:T(8,128)(2,1)}, bf16[4,5...) while((s32[]{:T(128)}, ...), condition=%wide.region_12.13_spmd.clone, body=%wide.region_10.12_spmd.clone.sunk | while | flops 340655104 | bytes 58091296 | solution.py:240
  1147.0 18.6 reduce-scatter.25.cloned.1.call-done
  1172.5 31.9 %reduce-scatter.27.cloned.1.call-done = bf16[128,2048]{1,0:T(8,128)(2,1)} async-done(((bf16[512,2048]{1,0:T(8,128)(2,1)}), bf16[128,2048]{1,0:T(8,128)(2,1)}) %reduce-scatter.27.cloned.1.call-update) | async-done | bytes 524304
  1229.1 16.6 convolution_convert_fusion.1
  1245.8 48.8 %reduce-scatter.15.cloned.1.call-done = bf16[512,2048]{1,0:T(8,128)(2,1)} async-done(((bf16[2048,2048]{1,0:T(8,128)(2,1)}), bf16[512,2048]{1,0:T(8,128)(2,1)}) %reduce-scatter.15.cloned.1.call-update) | async-done | bytes 2097168 | tf_op jit(solution)/shard_map/reduce_scatter | solution.py:289
  1294.5 89.6 %reduce-scatter.21.cloned.1.call-done = bf16[512,2048]{1,0:T(8,128)(2,1)} async-done(((bf16[2048,2048]{1,0:T(8,128)(2,1)}), bf16[512,2048]{1,0:T(8,128)(2,1)}) %reduce-scatter.21.cloned.1.call-update) | async-done | bytes 2097168 | tf_op jit(solution)/shard_map/reduce_scatter | solution.py:307
  1384.2 90.1 %reduce-scatter.17.cloned.1.call-done = bf16[512,2048]{1,0:T(8,128)(2,1)} async-done(((bf16[2048,2048]{1,0:T(8,128)(2,1)}), bf16[512,2048]{1,0:T(8,128)(2,1)}) %reduce-scatter.17.cloned.1.call-update) | async-done | bytes 2097168 | tf_op jit(solution)/shard_map/reduce_scatter | solution.py:295
  1474.2 89.6 %reduce-scatter.19.cloned.1.call-done = bf16[512,2048]{1,0:T(8,128)(2,1)} async-done(((bf16[2048,2048]{1,0:T(8,128)(2,1)}), bf16[512,2048]{1,0:T(8,128)(2,1)}) %reduce-scatter.19.cloned.1.call-update) | async-done | bytes 2097168 | tf_op jit(solution)/shard_map/reduce_scatter | solution.py:301
  1563.9 291.6 %reduce-scatter.23.cloned.1.call-done = bf16[2048,2048]{1,0:T(8,128)(2,1)} async-done(((bf16[2048,8192]{1,0:T(8,128)(2,1)}), bf16[2048,2048]{1,0:T(8,128)(2,1)}) %reduce-scatter.23.cloned.1.call-update) | async-done | bytes 8388624 | tf_op jit(solution)/shard_map/reduce_scatter | solution.py:187
  1855.5 291.9 %reduce-scatter.29.cloned.1.call-done = bf16[2048,2048]{1,0:T(8,128)(2,1)} async-done(((bf16[8192,2048]{1,0:T(8,128)(2,1)}), bf16[2048,2048]{1,0:T(8,128)(2,1)}) %reduce-scatter.29.cloned.1.call-update) | async-done | bytes 8388624
  2164.9 18.0 fusion.52
  2213.1 28.0 %all-reduce.10 = (bf16[512]{0:T(512)(128)(2,1)S(1)}, bf16[512]{0:T(512)(128)(2,1)S(1)}, bf16[512]{0:T(512)(128)(2,1)S(1)}, bf16[512]{0:T(512)(128)(2,1)S(1)}, bf...) all-reduce(bf16[512]{0:T(512)(128)(2,1)S(1)} %dynamic-slice.1, ...), channel_id=1, replica_groups=mesh['replica'=8,'group'=4] {'replica'}, use_global_device_ids=true, to_apply=%region_19.20 | all-reduce | flops 6144 | bytes 24576 | tf_op jit(solution)/shard_map/psum | solution.py:324
  2247.6 397.6 %all-reduce.15.cloned.1.call-done = (bf16[512,2048]{1,0:T(8,128)(2,1)}, bf16[512,2048]{1,0:T(8,128)(2,1)}, bf16[512,2048]{1,0:T(8,128)(2,1)}, bf16[512,2048]{1,0...) async-done(((bf16[512,2048]{1,0:T(8,128)(2,1)}, bf16[512,2048]{1,0:T(8,128)(2,1)}, bf16[512,2048]{1,0:T(8,128)(2,1)}, bf16[512,2048]{1,0:T(8,128)(2,1)}, ...) | async-done | bytes 25165840 | tf_op jit(solution)/shard_map/psum | solution.py:326
  (292 shorter events, 315.1 us)
Async XLA Ops:
  7.2 19.9 copy-start.24
  7.2 27.1 %copy-start = (bf16[128,2048]{1,0:T(8,128)(2,1)S(1)}, bf16[128,2048]{1,0:T(8,128)(2,1)}, u32[]{:S(2)}) copy-start(bf16[128,2048]{1,0:T(8,128)(2,1)} %param.23) | copy-start | bytes 1572868
  7.2 93.1 %all-gather.17.cloned.1.call-start = ((), (), s32[]{:S(2)}) async-start(), calls=%async_computation.8 | async-start | bytes 10485760 | tf_op jit(solution)/shard_map/all_gather | solution.py:116
  8.0 181.9 %all-gather.23.cloned.1.call-start = ((), (), s32[]{:S(2)}) async-start(), calls=%async_computation.11 | async-start | bytes 10485760 | tf_op jit(solution)/shard_map/all_gather | solution.py:115
  8.7 270.9 %all-gather.21.cloned.1.call-start = ((), (), s32[]{:S(2)}) async-start(), calls=%async_computation.10 | async-start | bytes 10485760 | tf_op jit(solution)/shard_map/all_gather | solution.py:114
  9.4 307.7 %all-gather.19.cloned.1.call-start = ((), (), s32[]{:S(2)}) async-start(), calls=%async_computation.9 | async-start | bytes 2621440 | tf_op jit(solution)/shard_map/all_gather | solution.py:134
  105.9 248.9 %all-gather.25.cloned.1.call-start = ((), (), s32[]{:S(2)}) async-start(), calls=%async_computation.12 | async-start | bytes 2621440 | tf_op jit(solution)/shard_map/all_gather | solution.py:133
  195.4 248.8 %all-gather.27.cloned.1.call-start = ((), (), s32[]{:S(2)}) async-start(), calls=%async_computation.13 | async-start | bytes 10485760 | tf_op jit(solution)/shard_map/all_gather | solution.py:117
  195.9 547.3 %all-gather.29.cloned.1.call-start = ((), (), s32[]{:S(2)}) async-start(), calls=%async_computation.14 | async-start | bytes 41943040 | tf_op jit(solution)/shard_map/all_gather | solution.py:160
  196.7 25.1 copy-start.27
  196.7 32.2 %copy-start.28 = (bf16[512]{0:T(512)(128)(2,1)S(1)}, bf16[512]{0:T(512)(128)(2,1)}, u32[]{:S(2)}) copy-start(bf16[512]{0:T(512)(128)(2,1)} %param.35) | copy-start | bytes 3076
  196.7 40.3 %copy-start.30 = (s32[128]{0:T(128)S(1)}, s32[128]{0:T(128)}, u32[]{:S(2)}) copy-start(s32[128]{0:T(128)} %param.25) | copy-start | bytes 1540
  196.8 845.6 %all-gather.31.cloned.1.call-start = ((), (), s32[]{:S(2)}) async-start(), calls=%async_computation.15 | async-start | bytes 41943040 | tf_op jit(solution)/shard_map/all_gather | solution.py:162
  197.5 968.0 %reduce-scatter.25.cloned.1.call-start = ((), (), s32[]{:S(2)}) async-start(), calls=%async_computation.21 | async-start | bytes 2621440
  1130.2 74.2 %reduce-scatter.27.cloned.1.call-start = ((), (), s32[]{:S(2)}) async-start(), calls=%async_computation.22 | async-start | bytes 2621440
  1134.2 160.3 %reduce-scatter.15.cloned.1.call-start = ((), (), s32[]{:S(2)}) async-start(), calls=%async_computation.16 | async-start | bytes 10485760 | tf_op jit(solution)/shard_map/reduce_scatter | solution.py:289
  1140.2 244.0 %reduce-scatter.21.cloned.1.call-start = ((), (), s32[]{:S(2)}) async-start(), calls=%async_computation.19 | async-start | bytes 10485760 | tf_op jit(solution)/shard_map/reduce_scatter | solution.py:307
  1146.9 327.3 %reduce-scatter.17.cloned.1.call-start = ((), (), s32[]{:S(2)}) async-start(), calls=%async_computation.17 | async-start | bytes 10485760 | tf_op jit(solution)/shard_map/reduce_scatter | solution.py:295
  1172.5 391.4 %reduce-scatter.19.cloned.1.call-start = ((), (), s32[]{:S(2)}) async-start(), calls=%async_computation.18 | async-start | bytes 10485760 | tf_op jit(solution)/shard_map/reduce_scatter | solution.py:301
  1211.2 644.3 %reduce-scatter.23.cloned.1.call-start = ((), (), s32[]{:S(2)}) async-start(), calls=%async_computation.20 | async-start | bytes 41943040 | tf_op jit(solution)/shard_map/reduce_scatter | solution.py:187
  1228.1 919.2 %reduce-scatter.29.cloned.1.call-start = ((), (), s32[]{:S(2)}) async-start(), calls=%async_computation.23 | async-start | bytes 41943040
  1245.7 1399.5 %all-reduce.15.cloned.1.call-start = ((), (), s32[]{:S(2)}) async-start(), calls=%async_computation.24 | async-start | bytes 50331648 | tf_op jit(solution)/shard_map/psum | solution.py:326
  2164.8 18.1 copy-start.9
  2189.5 56.9 %copy-start.12 = (f32[128,2048]{1,0:T(8,128)S(1)}, f32[128,2048]{1,0:T(8,128)}, u32[]{:S(2)}) copy-start(f32[128,2048]{1,0:T(8,128)} %get-tuple-element.224) | copy-start | bytes 3145732
  (49 other events, 125.0 us)
Sparse Core Ops, SparseCore 0:
  9.9 90.3 all-gather.16
  102.2 87.5 all-gather.22
  191.7 87.8 all-gather.20
  281.8 35.3 all-gather.18
  319.5 35.2 all-gather.24
  356.5 87.5 all-gather.26
  446.0 297.2 all-gather.28
  745.1 297.2 all-gather.30
  1130.3 35.1 reduce-scatter.24
  1169.2 35.1 reduce-scatter.26
  1208.1 86.3 reduce-scatter.14
  1297.7 86.3 reduce-scatter.20
  1387.8 86.3 reduce-scatter.16
  1477.4 86.3 reduce-scatter.18
  1566.8 288.6 reduce-scatter.22
  1858.7 288.6 reduce-scatter.28
  2150.5 494.6 all-reduce.14
where the time goes:
time: 2690 us
  waiting for transfers between devices  2250 us (84%)
  matrix products  210 us (8%)
  blocking collectives  116 us (4%)
  other arithmetic  50.9 us (2%)
  local copies, waits for them, and re-layouts  39.5 us (1%)
    psum x1, waiting for transfers between devices, shards(): lax.psum(query_wgrad.astype(jnp.bfloat16), 'replica').astype(jnp.float32)  398 us
    unnamed x20, waiting for transfers between devices  346 us
    all_gather x1, waiting for transfers between devices, shards(): lax.all_gather(up_weight, 'group', axis=1, tiled=True)  293 us
    reduce_scatter x1, waiting for transfers between devices, shards(): lax.psum_scatter(matmul(ffn_in.T, pre_grad).astype(jnp.bfloat16), 'group'...  292 us
    all_gather x1, waiting for transfers between devices, shards(): lax.all_gather(down_weight, 'group', axis=0, tiled=True)  278 us
    dot_general x18, matrix products, matmul(): return jnp.dot(left, right, preferred_element_type=jnp.float32)  182 us
    reduce_scatter x1, waiting for transfers between devices, shards(): lax.psum_scatter(matmul(attn_in.T, key_grad).astype(jnp.bfloat16), 'group...  90.1 us
    reduce_scatter x1, waiting for transfers between devices, shards(): lax.psum_scatter(matmul(attn_in.T, value_grad).astype(jnp.bfloat16), 'gro...  89.6 us
  transfers between devices with their start and end apart: 17, of which 17 were waited for; matrix products, arithmetic and copies ran while one was open for 6% of the time, Pallas kernels for 0%

commit v1 on v0

--- a/solution.py
+++ b/solution.py
@@ -323,7 +323,9 @@
     totals = (
         lax.psum(pre_gain_grad.astype(jnp.bfloat16), "replica").astype(jnp.float32),
         lax.psum(pre_shift_grad.astype(jnp.bfloat16), "replica").astype(jnp.float32),
-        lax.psum(query_wgrad.astype(jnp.bfloat16), "replica").astype(jnp.float32),
+        jnp.sum(lax.all_gather(query_wgrad.astype(jnp.bfloat16), "replica"), axis=0).astype(
+            jnp.float32
+        ),
         lax.psum(query_bgrad.astype(jnp.bfloat16), "replica").astype(jnp.float32),
         lax.psum(key_wgrad.astype(jnp.bfloat16), "replica").astype(jnp.float32),
         lax.psum(value_wgrad.astype(jnp.bfloat16), "replica").astype(jnp.float32),

time: 2690 us -> 2800 us (1.041)
  waiting for transfers between devices: 2250 us -> 2350 us
    all_gather x0 -> x1, waiting for transfers between devices: none -> 49.1 us  [shards(): lax.all_gather(query_wgrad.astype(jnp.bfloat16), 'replica')]
    psum x1, waiting for transfers between devices: 398 us -> 443 us  [shards(): lax.psum(key_wgrad.astype(jnp.bfloat16), 'replica').astype(jnp.float32)]
    unnamed x20 -> x21, waiting for transfers between devices: 346 us -> 347 us
  transfers between devices with their start and end apart: 17 -> 18, of which waited for: 17 -> 18; matrix products, arithmetic and copies ran while one was open for 6% -> 7% of each run, Pallas kernels for 0% -> 0%
where the time goes in v1:
time: 2800 us
  waiting for transfers between devices  2350 us (84%)
  matrix products  212 us (8%)
  blocking collectives  118 us (4%)
  other arithmetic  60.7 us (2%)
  local copies, waits for them, and re-layouts  39.6 us (1%)
    psum x1, waiting for transfers between devices, shards(): lax.psum(key_wgrad.astype(jnp.bfloat16), 'replica').astype(jnp.float32)  443 us
    unnamed x21, waiting for transfers between devices  347 us
    all_gather x1, waiting for transfers between devices, shards(): lax.all_gather(up_weight, 'group', axis=1, tiled=True)  293 us
    reduce_scatter x1, waiting for transfers between devices, shards(): lax.psum_scatter(matmul(ffn_in.T, pre_grad).astype(jnp.bfloat16), 'group'...  292 us
    all_gather x1, waiting for transfers between devices, shards(): lax.all_gather(down_weight, 'group', axis=0, tiled=True)  278 us
    dot_general x18, matrix products, matmul(): return jnp.dot(left, right, preferred_element_type=jnp.float32)  183 us
    reduce_scatter x1, waiting for transfers between devices, shards(): lax.psum_scatter(matmul(attn_in.T, key_grad).astype(jnp.bfloat16), 'group...  90.1 us
    reduce_scatter x1, waiting for transfers between devices, shards(): lax.psum_scatter(matmul(attn_in.T, value_grad).astype(jnp.bfloat16), 'gro...  89.6 us
  transfers between devices with their start and end apart: 18, of which 18 were waited for; matrix products, arithmetic and copies ran while one was open for 7% of the time, Pallas kernels for 0%

profile of v1, /device:TPU:0, one launch (start us, length us, event | category | flops | bytes accessed | tf_op | source)
XLA Modules:
  0.0 2795.7 jit_solution(13291426279189481237)
XLA Ops:
  34.8 65.6 %all-gather.19.cloned.1.call-done = bf16[2048,2048]{1,0:T(8,128)(2,1)} async-done(((bf16[512,2048]{1,0:T(8,128)(2,1)}), bf16[2048,2048]{1,0:T(8,128)(2,1)}) %all-gather.19.cloned.1.call-update) | async-done | bytes 8388624 | tf_op jit(solution)/shard_map/all_gather | solution.py:116
  105.9 83.9 %all-gather.25.cloned.1.call-done = bf16[2048,2048]{1,0:T(8,128)(2,1)} async-done(((bf16[512,2048]{1,0:T(8,128)(2,1)}), bf16[2048,2048]{1,0:T(8,128)(2,1)}) %all-gather.25.cloned.1.call-update) | async-done | bytes 8388624 | tf_op jit(solution)/shard_map/all_gather | solution.py:115
  237.1 42.5 %all-gather.23.cloned.1.call-done = bf16[2048,2048]{1,0:T(8,128)(2,1)} async-done(((bf16[512,2048]{1,0:T(8,128)(2,1)}), bf16[2048,2048]{1,0:T(8,128)(2,1)}) %all-gather.23.cloned.1.call-update) | async-done | bytes 8388624 | tf_op jit(solution)/shard_map/all_gather | solution.py:114
  284.6 32.6 %all-gather.21.cloned.1.call-done = bf16[512,2048]{1,0:T(8,128)(2,1)} async-done(((bf16[128,2048]{1,0:T(8,128)(2,1)}), bf16[512,2048]{1,0:T(8,128)(2,1)}) %all-gather.21.cloned.1.call-update) | async-done | bytes 2097168 | tf_op jit(solution)/shard_map/all_gather | solution.py:134
  321.3 33.5 %all-gather.27.cloned.1.call-done = bf16[512,2048]{1,0:T(8,128)(2,1)} async-done(((bf16[128,2048]{1,0:T(8,128)(2,1)}), bf16[512,2048]{1,0:T(8,128)(2,1)}) %all-gather.27.cloned.1.call-update) | async-done | bytes 2097168 | tf_op jit(solution)/shard_map/all_gather | solution.py:133
  374.4 69.8 %all-gather.29.cloned.1.call-done = bf16[2048,2048]{1,0:T(8,128)(2,1)} async-done(((bf16[512,2048]{1,0:T(8,128)(2,1)}), bf16[2048,2048]{1,0:T(8,128)(2,1)}) %all-gather.29.cloned.1.call-update) | async-done | bytes 8388624 | tf_op jit(solution)/shard_map/all_gather | solution.py:117
  450.4 292.8 %all-gather.31.cloned.1.call-done = bf16[2048,8192]{1,0:T(8,128)(2,1)} async-done(((bf16[2048,2048]{1,0:T(8,128)(2,1)}), bf16[2048,8192]{1,0:T(8,128)(2,1)}) %all-gather.31.cloned.1.call-update) | async-done | bytes 33554448 | tf_op jit(solution)/shard_map/all_gather | solution.py:160
  743.3 20.8 convolution_add_fusion
  764.0 278.3 %all-gather.33.cloned.1.call-done = bf16[8192,2048]{1,0:T(8,128)(2,1)} async-done(((bf16[2048,2048]{1,0:T(8,128)(2,1)}), bf16[8192,2048]{1,0:T(8,128)(2,1)}) %all-gather.33.cloned.1.call-update) | async-done | bytes 33554448 | tf_op jit(solution)/shard_map/all_gather | solution.py:162
  1042.3 18.8 fusion.81
  1061.2 19.7 multiply_reduce_fusion.1
  1095.0 31.3 %while.29 = (s32[]{:T(128)}, bf16[4,128,8,64]{1,3,2,0:T(8,128)(2,1)}, bf16[4,512,8,64]{1,3,2,0:T(8,128)(2,1)}, bf16[4,512,8,64]{1,3,2,0:T(8,128)(2,1)}, bf16[4,5...) while((s32[]{:T(128)}, ...), condition=%wide.region_12.13_spmd.clone, body=%wide.region_10.12_spmd.clone.sunk | while | flops 340655104 | bytes 58091296 | solution.py:240
  1147.0 18.6 reduce-scatter.25.cloned.1.call-done
  1172.5 31.9 %reduce-scatter.27.cloned.1.call-done = bf16[128,2048]{1,0:T(8,128)(2,1)} async-done(((bf16[512,2048]{1,0:T(8,128)(2,1)}), bf16[128,2048]{1,0:T(8,128)(2,1)}) %reduce-scatter.27.cloned.1.call-update) | async-done | bytes 524304
  1245.7 48.8 %reduce-scatter.15.cloned.1.call-done = bf16[512,2048]{1,0:T(8,128)(2,1)} async-done(((bf16[2048,2048]{1,0:T(8,128)(2,1)}), bf16[512,2048]{1,0:T(8,128)(2,1)}) %reduce-scatter.15.cloned.1.call-update) | async-done | bytes 2097168 | tf_op jit(solution)/shard_map/reduce_scatter | solution.py:289
  1294.6 89.6 %reduce-scatter.21.cloned.1.call-done = bf16[512,2048]{1,0:T(8,128)(2,1)} async-done(((bf16[2048,2048]{1,0:T(8,128)(2,1)}), bf16[512,2048]{1,0:T(8,128)(2,1)}) %reduce-scatter.21.cloned.1.call-update) | async-done | bytes 2097168 | tf_op jit(solution)/shard_map/reduce_scatter | solution.py:307
  1384.1 90.1 %reduce-scatter.17.cloned.1.call-done = bf16[512,2048]{1,0:T(8,128)(2,1)} async-done(((bf16[2048,2048]{1,0:T(8,128)(2,1)}), bf16[512,2048]{1,0:T(8,128)(2,1)}) %reduce-scatter.17.cloned.1.call-update) | async-done | bytes 2097168 | tf_op jit(solution)/shard_map/reduce_scatter | solution.py:295
  1474.2 89.6 %reduce-scatter.19.cloned.1.call-done = bf16[512,2048]{1,0:T(8,128)(2,1)} async-done(((bf16[2048,2048]{1,0:T(8,128)(2,1)}), bf16[512,2048]{1,0:T(8,128)(2,1)}) %reduce-scatter.19.cloned.1.call-update) | async-done | bytes 2097168 | tf_op jit(solution)/shard_map/reduce_scatter | solution.py:301
  1563.8 291.6 %reduce-scatter.23.cloned.1.call-done = bf16[2048,2048]{1,0:T(8,128)(2,1)} async-done(((bf16[2048,8192]{1,0:T(8,128)(2,1)}), bf16[2048,2048]{1,0:T(8,128)(2,1)}) %reduce-scatter.23.cloned.1.call-update) | async-done | bytes 8388624 | tf_op jit(solution)/shard_map/reduce_scatter | solution.py:187
  1855.5 291.9 %reduce-scatter.29.cloned.1.call-done = bf16[2048,2048]{1,0:T(8,128)(2,1)} async-done(((bf16[8192,2048]{1,0:T(8,128)(2,1)}), bf16[2048,2048]{1,0:T(8,128)(2,1)}) %reduce-scatter.29.cloned.1.call-update) | async-done | bytes 8388624
  2166.3 18.1 fusion.52
  2214.5 30.3 %all-reduce.10 = (bf16[512]{0:T(512)(128)(2,1)S(1)}, bf16[512]{0:T(512)(128)(2,1)S(1)}, bf16[512]{0:T(512)(128)(2,1)S(1)}, bf16[512]{0:T(512)(128)(2,1)S(1)}, bf...) all-reduce(bf16[512]{0:T(512)(128)(2,1)S(1)} %dynamic-slice.1, ...), channel_id=1, replica_groups=mesh['replica'=8,'group'=4] {'replica'}, use_global_device_ids=true, to_apply=%region_19.20 | all-reduce | flops 6144 | bytes 24576 | tf_op jit(solution)/shard_map/psum | solution.py:324
  2251.3 49.1 %all-gather.35.cloned.1.call-done = bf16[4096,2048]{1,0:T(8,128)(2,1)} async-done(((bf16[512,2048]{1,0:T(8,128)(2,1)}), bf16[4096,2048]{1,0:T(8,128)(2,1)}) %all-gather.35.cloned.1.call-update) | async-done | bytes 16777232 | tf_op jit(solution)/shard_map/all_gather | solution.py:326
  2312.8 442.9 %all-reduce.15.cloned.1.call-done = (bf16[512,2048]{1,0:T(8,128)(2,1)}, bf16[512,2048]{1,0:T(8,128)(2,1)}, bf16[512,2048]{1,0:T(8,128)(2,1)}, bf16[2048,2048]{1,0:T(8,128)(2,1)}, bf16[2048,2048]{1,0:T(8,128)(2,1)}) async-done(((bf16[512,2048]{1,0:T(8,128)(2,1)}, bf16[512,2048]{1,0:T(8,128)(2,1)}, bf16[512,2048]{1,0:T(8,128)(2,1)}, bf16[2048,2048]{1,0:T(8,128)(2,1)}, bf16[2048,2048]{1,0:T(8,128)(2,1)}), ...) | async-done | bytes 23068688 | tf_op jit(solution)/shard_map/psum | solution.py:330
  (294 shorter events, 342.9 us)
Async XLA Ops:
  7.2 19.9 copy-start.23
  7.2 27.1 copy-start
  7.2 93.1 %all-gather.19.cloned.1.call-start = ((), (), s32[]{:S(2)}) async-start(), calls=%async_computation.8 | async-start | bytes 10485760 | tf_op jit(solution)/shard_map/all_gather | solution.py:116
  8.0 181.9 %all-gather.25.cloned.1.call-start = ((), (), s32[]{:S(2)}) async-start(), calls=%async_computation.11 | async-start | bytes 10485760 | tf_op jit(solution)/shard_map/all_gather | solution.py:115
  8.7 270.9 %all-gather.23.cloned.1.call-start = ((), (), s32[]{:S(2)}) async-start(), calls=%async_computation.10 | async-start | bytes 10485760 | tf_op jit(solution)/shard_map/all_gather | solution.py:114
  9.4 307.7 %all-gather.21.cloned.1.call-start = ((), (), s32[]{:S(2)}) async-start(), calls=%async_computation.9 | async-start | bytes 2621440 | tf_op jit(solution)/shard_map/all_gather | solution.py:134
  105.9 248.9 %all-gather.27.cloned.1.call-start = ((), (), s32[]{:S(2)}) async-start(), calls=%async_computation.12 | async-start | bytes 2621440 | tf_op jit(solution)/shard_map/all_gather | solution.py:133
  195.4 248.8 %all-gather.29.cloned.1.call-start = ((), (), s32[]{:S(2)}) async-start(), calls=%async_computation.13 | async-start | bytes 10485760 | tf_op jit(solution)/shard_map/all_gather | solution.py:117
  195.9 547.3 %all-gather.31.cloned.1.call-start = ((), (), s32[]{:S(2)}) async-start(), calls=%async_computation.14 | async-start | bytes 41943040 | tf_op jit(solution)/shard_map/all_gather | solution.py:160
  196.7 25.1 copy-start.26
  196.7 32.2 %copy-start.27 = (bf16[512]{0:T(512)(128)(2,1)S(1)}, bf16[512]{0:T(512)(128)(2,1)}, u32[]{:S(2)}) copy-start(bf16[512]{0:T(512)(128)(2,1)} %param.35) | copy-start | bytes 3076
  196.7 40.3 %copy-start.29 = (s32[128]{0:T(128)S(1)}, s32[128]{0:T(128)}, u32[]{:S(2)}) copy-start(s32[128]{0:T(128)} %param.25) | copy-start | bytes 1540
  196.8 845.6 %all-gather.33.cloned.1.call-start = ((), (), s32[]{:S(2)}) async-start(), calls=%async_computation.15 | async-start | bytes 41943040 | tf_op jit(solution)/shard_map/all_gather | solution.py:162
  197.5 968.0 %reduce-scatter.25.cloned.1.call-start = ((), (), s32[]{:S(2)}) async-start(), calls=%async_computation.22 | async-start | bytes 2621440
  1130.2 74.2 %reduce-scatter.27.cloned.1.call-start = ((), (), s32[]{:S(2)}) async-start(), calls=%async_computation.23 | async-start | bytes 2621440
  1134.2 160.3 %reduce-scatter.15.cloned.1.call-start = ((), (), s32[]{:S(2)}) async-start(), calls=%async_computation.16 | async-start | bytes 10485760 | tf_op jit(solution)/shard_map/reduce_scatter | solution.py:289
  1140.2 244.0 %reduce-scatter.21.cloned.1.call-start = ((), (), s32[]{:S(2)}) async-start(), calls=%async_computation.19 | async-start | bytes 10485760 | tf_op jit(solution)/shard_map/reduce_scatter | solution.py:307
  1146.9 327.3 %reduce-scatter.17.cloned.1.call-start = ((), (), s32[]{:S(2)}) async-start(), calls=%async_computation.17 | async-start | bytes 10485760 | tf_op jit(solution)/shard_map/reduce_scatter | solution.py:295
  1172.5 391.4 %reduce-scatter.19.cloned.1.call-start = ((), (), s32[]{:S(2)}) async-start(), calls=%async_computation.18 | async-start | bytes 10485760 | tf_op jit(solution)/shard_map/reduce_scatter | solution.py:301
  1211.2 644.3 %reduce-scatter.23.cloned.1.call-start = ((), (), s32[]{:S(2)}) async-start(), calls=%async_computation.20 | async-start | bytes 41943040 | tf_op jit(solution)/shard_map/reduce_scatter | solution.py:187
  1228.1 919.3 %reduce-scatter.29.cloned.1.call-start = ((), (), s32[]{:S(2)}) async-start(), calls=%async_computation.24 | async-start | bytes 41943040
  1245.7 1054.8 %all-gather.35.cloned.1.call-start = ((), (), s32[]{:S(2)}) async-start(), calls=%async_computation.21 | async-start | bytes 18874368 | tf_op jit(solution)/shard_map/all_gather | solution.py:326
  1294.5 1461.2 %all-reduce.15.cloned.1.call-start = ((), (), s32[]{:S(2)}) async-start(), calls=%async_computation.25 | async-start | bytes 46137344 | tf_op jit(solution)/shard_map/psum | solution.py:330
  2191.1 59.0 %copy-start.12 = (f32[128,2048]{1,0:T(8,128)S(1)}, f32[128,2048]{1,0:T(8,128)}, u32[]{:S(2)}) copy-start(f32[128,2048]{1,0:T(8,128)} %get-tuple-element.223) | copy-start | bytes 3145732
  (49 other events, 140.6 us)
Sparse Core Ops, SparseCore 0:
  9.9 90.3 all-gather.18
  102.2 87.5 all-gather.24
  191.7 87.8 all-gather.22
  281.8 35.3 all-gather.20
  319.5 35.2 all-gather.26
  356.5 87.5 all-gather.28
  446.0 297.2 all-gather.30
  745.1 297.2 all-gather.32
  1130.3 35.1 reduce-scatter.24
  1169.2 35.1 reduce-scatter.26
  1208.1 86.3 reduce-scatter.14
  1297.7 86.3 reduce-scatter.20
  1387.8 86.3 reduce-scatter.16
  1477.4 86.3 reduce-scatter.18
  1566.8 288.6 reduce-scatter.22
  1858.7 288.6 reduce-scatter.28
  2148.8 151.6 all-gather.34
  2303.4 452.2 all-reduce.14
